TPU v7x, 32 devices: a whole 2x2x4 slice. The times are simulated.
32 devices in a mesh: seq: 4 (over y, x), grp: 2 (over core), wsh: 4 (over z).
Axes of the slice: x: 2, y: 2, z: 4, core: 2. Of those that a mesh axis runs over, the one named last changes fastest.
Arguments:
- hidden: bfloat16 [8, 1024, 1536], P(('grp', 'wsh'), 'seq'), may hold values from -6 to 6
- norm_gain: bfloat16 [1536], P('wsh'), may hold values from 0.5 to 1.5
- in_weight: bfloat16 [1536, 6448], P('wsh'), may hold values from -0.15625 to 0.15625
- conv_weight: bfloat16 [3328, 4], P('wsh'), may hold values from -3 to 3
- conv_bias: bfloat16 [3328], P('wsh'), may hold values from -3 to 3
- dt_bias: bfloat16 [48], P('wsh'), may hold values from -13 to -3
- a_log: bfloat16 [48], P('wsh'), may hold values from 0 to 2.7
- skip_gain: bfloat16 [48], P('wsh'), may hold values from 0.5 to 2
- gate_gain: bfloat16 [3072], P('wsh'), may hold values from 0.5 to 1.5
- out_weight: bfloat16 [3072, 1536], P('wsh'), may hold values from -0.109375 to 0.109375
- d_out: bfloat16 [8, 1024, 1536], P(('grp', 'wsh'), 'seq'), may hold values from -6 to 6
Outputs:
- layer_out: bfloat16 [8, 1024, 1536], P(('grp', 'wsh'), 'seq')
- d_hidden: bfloat16 [8, 1024, 1536], P(('grp', 'wsh'), 'seq')
- grad_norm_gain: float32 [1536], P('wsh')
- grad_in_weight: float32 [1536, 6448], P('wsh')
- grad_conv_weight: float32 [3328, 4], P('wsh')
- grad_conv_bias: float32 [3328], P('wsh')
- grad_dt_bias: float32 [48], P('wsh')
- grad_a_log: float32 [48], P('wsh')
- grad_skip_gain: float32 [48], P('wsh')
- grad_gate_gain: float32 [3072], P('wsh')
- grad_out_weight: float32 [3072, 1536], P('wsh')
All inputs are finite; a program needn't handle non-finite values.
Results may differ from a plain program's by a relative error of at most 0.0091.
Values may be sent and summed in bfloat16 or wider, within the bound.
No kernel may reach another device: no remote copies, remote signals or barrier semaphores. Data moves between devices by JAX's collectives and lax.ppermute only.
A program may use at most 320 MiB of HBM per device.

v0:
```python
import jax
import jax.numpy as jnp
from jax import lax
from jax.sharding import PartitionSpec as P

DI = 3072
KCONV = 4
QCH = 256
CONVC = 3328
epsilon = 1e-05
highest = lax.Precision.HIGHEST


def shifted(block, axis, distance):
    devices = range(lax.axis_size(axis))
    route = [(i - distance, i) for i in devices if i - distance in devices]
    return lax.ppermute(block, axis, route)


def rms_apply(values, gain_vec):
    inverse = lax.rsqrt(jnp.mean(values * values, axis=-1, keepdims=True) + epsilon)
    return values * inverse * gain_vec[None, :]


def gated_apply(mixer_out, gate_in, gain_vec):
    product = mixer_out * jax.nn.silu(gate_in)
    inverse = lax.rsqrt(jnp.mean(product * product, axis=-1, keepdims=True) + epsilon)
    return product * inverse * gain_vec[None, :]


def conv_apply(padded, weight, bias_vec):
    tap_count = weight.shape[1]
    row_count = padded.shape[0] - tap_count + 1
    summed = jnp.zeros((row_count, padded.shape[1]), jnp.float32) + bias_vec[None, :]
    for offset in range(tap_count):
        summed = summed + padded[offset : offset + row_count] * weight[:, offset][None, :]
    return jax.nn.silu(summed)


def ssd_apply(x_values, dt_raw, b_and_c, dt_bias, a_log, skip_gain):
    length, head_count = dt_raw.shape
    head_size = x_values.shape[1] // head_count
    state_count = b_and_c.shape[1] // 2
    block_count = length // QCH
    dt_value = jax.nn.softplus(dt_raw + dt_bias[None, :])
    log_rate = -jnp.exp(a_log)[None, :] * dt_value
    causal = (jnp.arange(QCH)[:, None] >= jnp.arange(QCH)[None, :]).astype(jnp.float32)
    x_blocks = x_values.reshape(block_count, QCH, head_count, head_size)
    dt_blocks = dt_value.reshape(block_count, QCH, head_count)
    rate_blocks = log_rate.reshape(block_count, QCH, head_count)
    b_blocks = b_and_c[:, :state_count].reshape(block_count, QCH, state_count)
    c_blocks = b_and_c[:, state_count:].reshape(block_count, QCH, state_count)

    def advance(carried, pieces):
        x_block, dt_block, rate_block, b_block, c_block = pieces
        cumulated = jnp.cumsum(rate_block, axis=0)
        gram_matrix = jnp.dot(c_block, b_block.T, precision=highest)
        spread = cumulated.T[:, :, None] - cumulated.T[:, None, :]
        mixing = (
            jnp.exp(spread * causal[None])
            * causal[None]
            * gram_matrix[None]
            * dt_block.T[:, None, :]
        )
        result = jnp.einsum("hts,shp->thp", mixing, x_block, precision=highest)
        result = (
            result
            + jnp.einsum("tn,hnp->thp", c_block, carried, precision=highest)
            * jnp.exp(cumulated)[:, :, None]
        )
        final_sum = cumulated[-1]
        tail_weight = jnp.exp(final_sum[None, :] - cumulated) * dt_block
        carried = carried * jnp.exp(final_sum)[:, None, None] + jnp.einsum(
            "sn,sh,shp->hnp", b_block, tail_weight, x_block, precision=highest
        )
        return (carried, result)

    initial = jnp.zeros((head_count, state_count, head_size), jnp.float32)
    _, outputs = lax.scan(advance, initial, (x_blocks, dt_blocks, rate_blocks, b_blocks, c_blocks))
    return (
        outputs.reshape(length, head_count * head_size)
        + x_values * jnp.repeat(skip_gain, head_size)[None, :]
    )


def reduce_grads(grads):
    shares = (
        lax.psum_scatter(grads[0], "wsh", scatter_dimension=0, tiled=True),
        lax.psum_scatter(grads[1], "wsh", scatter_dimension=0, tiled=True),
        lax.psum_scatter(grads[2], "wsh", scatter_dimension=0, tiled=True),
        lax.psum_scatter(grads[3], "wsh", scatter_dimension=0, tiled=True),
        lax.psum_scatter(grads[4], "wsh", scatter_dimension=0, tiled=True),
        lax.psum_scatter(grads[5], "wsh", scatter_dimension=0, tiled=True),
        lax.psum_scatter(grads[6], "wsh", scatter_dimension=0, tiled=True),
        lax.psum_scatter(grads[7], "wsh", scatter_dimension=0, tiled=True),
        lax.psum_scatter(grads[8], "wsh", scatter_dimension=0, tiled=True),
    )
    return lax.psum(
        (
            shares[0],
            shares[1],
            shares[2],
            shares[3],
            shares[4],
            shares[5],
            shares[6],
            shares[7],
            shares[8],
        ),
        ("seq", "grp"),
    )


def body(
    hidden,
    norm_gain,
    in_weight,
    conv_weight,
    conv_bias,
    dt_bias,
    a_log,
    skip_gain,
    gate_gain,
    out_weight,
    d_out,
):
    gathered = (
        lax.all_gather(norm_gain, "wsh", axis=0, tiled=True),
        lax.all_gather(in_weight, "wsh", axis=0, tiled=True),
        lax.all_gather(conv_weight, "wsh", axis=0, tiled=True),
        lax.all_gather(conv_bias, "wsh", axis=0, tiled=True),
        lax.all_gather(dt_bias, "wsh", axis=0, tiled=True),
        lax.all_gather(a_log, "wsh", axis=0, tiled=True),
        lax.all_gather(skip_gain, "wsh", axis=0, tiled=True),
    )
    full_norm, full_in, full_conv, full_cbias, full_dtb, full_alog, full_skip = gathered
    tokens_f = hidden[0].astype(jnp.float32)
    cotangent = d_out[0]
    normed_f, rms_back = jax.vjp(rms_apply, tokens_f, full_norm.astype(jnp.float32))
    normed = lax.optimization_barrier(normed_f.astype(jnp.bfloat16))
    projected = lax.optimization_barrier(
        jnp.dot(normed, full_in, preferred_element_type=jnp.float32).astype(jnp.bfloat16)
    )
    gate_part = projected[:, :DI]
    conv_input = projected[:, DI : DI + CONVC]
    dt_part = projected[:, DI + CONVC :]
    rim_rows = shifted(conv_input[conv_input.shape[0] - (KCONV - 1) :], "seq", 1)
    padded = jnp.concatenate([rim_rows, conv_input], axis=0).astype(jnp.float32)
    conved_f, conv_back = jax.vjp(
        conv_apply, padded, full_conv.astype(jnp.float32), full_cbias.astype(jnp.float32)
    )
    conved = lax.optimization_barrier(conved_f.astype(jnp.bfloat16))
    x_heads, dt_heads = (
        lax.all_to_all(conved[:, :DI], "seq", split_axis=1, concat_axis=0, tiled=True),
        lax.all_to_all(dt_part, "seq", split_axis=1, concat_axis=0, tiled=True),
    )
    bc_whole = lax.all_gather(conved[:, DI:], "seq", axis=0, tiled=True)
    local_heads = dt_heads.shape[1]
    head_start = lax.axis_index("seq") * local_heads
    bias_local = lax.dynamic_slice_in_dim(full_dtb.astype(jnp.float32), head_start, local_heads)
    alog_local = lax.dynamic_slice_in_dim(full_alog.astype(jnp.float32), head_start, local_heads)
    skip_local = lax.dynamic_slice_in_dim(full_skip.astype(jnp.float32), head_start, local_heads)
    x_float = x_heads.astype(jnp.float32)
    dt_float = dt_heads.astype(jnp.float32)
    bc_float = bc_whole.astype(jnp.float32)
    y_heads = ssd_apply(x_float, dt_float, bc_float, bias_local, alog_local, skip_local).astype(
        jnp.bfloat16
    )
    y_tokens = lax.all_to_all(y_heads, "seq", split_axis=0, concat_axis=1, tiled=True)
    full_gate, full_out = (
        lax.all_gather(gate_gain, "wsh", axis=0, tiled=True),
        lax.all_gather(out_weight, "wsh", axis=0, tiled=True),
    )
    gated_f, gate_back = jax.vjp(
        gated_apply,
        y_tokens.astype(jnp.float32),
        gate_part.astype(jnp.float32),
        full_gate.astype(jnp.float32),
    )
    gated = gated_f.astype(jnp.bfloat16)
    layer_out = (tokens_f + jnp.dot(gated, full_out, preferred_element_type=jnp.float32)).astype(
        jnp.bfloat16
    )
    grad_out = jnp.einsum("td,te->de", gated, cotangent, preferred_element_type=jnp.float32)
    d_gated = lax.dot_general(
        cotangent, full_out, (((1,), (1,)), ((), ())), preferred_element_type=jnp.float32
    )
    d_mixer, d_gate_part, grad_gate = gate_back(d_gated)
    d_y_heads = lax.all_to_all(
        d_mixer.astype(jnp.bfloat16), "seq", split_axis=1, concat_axis=0, tiled=True
    )
    _, ssd_back = jax.vjp(
        ssd_apply, x_float, dt_float, bc_float, bias_local, alog_local, skip_local
    )
    d_x, d_dt, d_bc_part, grad_dtb, grad_alog, grad_skip = ssd_back(d_y_heads.astype(jnp.float32))
    d_bc = lax.psum_scatter(d_bc_part, "seq", scatter_dimension=0, tiled=True)
    d_x_tokens, d_dt_tokens = (
        lax.all_to_all(d_x.astype(jnp.bfloat16), "seq", split_axis=0, concat_axis=1, tiled=True),
        lax.all_to_all(d_dt.astype(jnp.bfloat16), "seq", split_axis=0, concat_axis=1, tiled=True),
    )
    d_conved = jnp.concatenate([d_x_tokens.astype(jnp.float32), d_bc], axis=1)
    d_padded, grad_conv, grad_cbias = conv_back(d_conved)
    rim_grad = shifted(d_padded[: KCONV - 1].astype(jnp.bfloat16), "seq", -1).astype(jnp.float32)
    own_rows = conv_input.shape[0]
    d_conv_input = d_padded[KCONV - 1 :] + jnp.concatenate(
        [jnp.zeros((own_rows - (KCONV - 1), CONVC), jnp.float32), rim_grad], axis=0
    )
    d_projected = jnp.concatenate(
        [d_gate_part, d_conv_input, d_dt_tokens.astype(jnp.float32)], axis=1
    ).astype(jnp.bfloat16)
    grad_in = jnp.einsum("td,tp->dp", normed, d_projected, preferred_element_type=jnp.float32)
    d_normed = lax.dot_general(
        d_projected, full_in, (((1,), (1,)), ((), ())), preferred_element_type=jnp.float32
    )
    d_tokens, grad_norm = rms_back(d_normed)
    d_hidden = (cotangent.astype(jnp.float32) + d_tokens).astype(jnp.bfloat16)
    all_heads = full_dtb.shape[0]
    placed_dtb = lax.dynamic_update_slice_in_dim(
        jnp.zeros((all_heads,), jnp.float32), grad_dtb, head_start, 0
    )
    placed_alog = lax.dynamic_update_slice_in_dim(
        jnp.zeros((all_heads,), jnp.float32), grad_alog, head_start, 0
    )
    placed_skip = lax.dynamic_update_slice_in_dim(
        jnp.zeros((all_heads,), jnp.float32), grad_skip, head_start, 0
    )
    reduced = reduce_grads(
        (
            grad_norm,
            grad_in,
            grad_conv,
            grad_cbias,
            placed_dtb,
            placed_alog,
            placed_skip,
            grad_gate,
            grad_out,
        )
    )
    return (
        layer_out[None],
        d_hidden[None],
        reduced[0],
        reduced[1],
        reduced[2],
        reduced[3],
        reduced[4],
        reduced[5],
        reduced[6],
        reduced[7],
        reduced[8],
    )


def solution(mesh):
    placed = (
        P(("grp", "wsh"), "seq", None),
        P("wsh"),
        P("wsh", None),
        P("wsh", None),
        P("wsh"),
        P("wsh"),
        P("wsh"),
        P("wsh"),
        P("wsh"),
        P("wsh", None),
        P(("grp", "wsh"), "seq", None),
    )
    return jax.shard_map(
        body,
        mesh=mesh,
        in_specs=placed,
        out_specs=(
            P(("grp", "wsh"), "seq", None),
            P(("grp", "wsh"), "seq", None),
            P("wsh"),
            P("wsh", None),
            P("wsh", None),
            P("wsh"),
            P("wsh"),
            P("wsh"),
            P("wsh"),
            P("wsh"),
            P("wsh", None),
        ),
        check_vma=False,
    )
```

profile of v0, /device:TPU:0, one launch (start us, length us, event | category | flops | bytes accessed | tf_op | source)
XLA Modules:
  0.0 2245.3 jit_solution(12582450332125656297)
XLA Ops:
  9.0 13.6 all-gather
  22.7 13.5 all-gather.1
  37.5 312.8 %all-gather.6.cloned.1.call-done = bf16[1536,6448]{0,1:T(8,128)(2,1)} async-done(((bf16[384,6448]{0,1:T(8,128)(2,1)}), bf16[1536,6448]{0,1:T(8,128)(2,1)}) %all-gather.6.cloned.1.call-update) | async-done | bytes 19808272 | tf_op jit(solution)/shard_map/all_gather | solution.py:129
  350.3 10.3 convolution_convert_fusion
  370.2 10.7 all-reduce.25
  389.6 6.9 multiply_convert_fusion
  404.4 26.2 %all_gather.36 = bf16[1024,256]{0,1:T(8,128)(2,1)S(1)} all-gather(bf16[256,256]{0,1:T(8,128)(2,1)S(1)} %slice.146), channel_id=1, replica_groups=mesh['seq'=4,'grp'=2,'wsh'=4] {'seq'}, dimensions={0}, use_global_device_ids=true | all-gather | bytes 655360 | tf_op jit(solution)/shard_map/all_gather | solution.py:157
  436.7 52.1 %while.86 = (s32[]{:T(128)}, f32[12,128,64]{1,2,0:T(8,128)}, f32[4,256,12,64]{1,3,2,0:T(8,128)}, f32[4,256,12]{1,2,0:T(8,128)}, f32[4,256,12]{1,2,0:T(8,128)S(1)...) while((s32[]{:T(128)}, f32[12,128,64]{1,2,0:T(8,128)}, ...), condition=%wide.region_4.5_spmd.clone.clone, body=%wide.region_1.4_spmd.clone.clone.sunk | while | flops 1313970176 | bytes 8233615 | solution.py:79
  497.3 19.0 all-gather.2
  521.5 8.7 multiply_reduce_fusion.4
  545.9 128.5 %while.87 = (s32[]{:T(128)}, f32[12,128,64]{1,2,0:T(8,128)}, f32[4,128,256]{1,2,0:T(8,128)}, f32[4,12,256,256]{3,2,1,0:T(8,128)}, f32[4,1,256,256]{3,2,1,0:T(8,1...) while((s32[]{:T(128)}, f32[12,128,64]{1,2,0:T(8,128)}, ...), condition=%wide.region_10.11_spmd.clone.clone, body=%wide.region_7.10_spmd.clone.clone.sunk | while | flops 709793792 | bytes 22214624 | solution.py:79
  572.1 5.3 multiply_dynamic-update-slice_fusion.3
  682.6 290.8 %while.88 = (s32[]{:T(128)}, f32[12,128,64]{1,2,0:T(8,128)S(1)}, f32[4,256,12,64]{1,3,2,0:T(8,128)}, f32[4,256,12]{1,2,0:T(8,128)}, f32[4,256,12]{1,2,0:T(8,128)...) while((s32[]{:T(128)}, f32[12,128,64]{1,2,0:T(8,128)S(1)}, ...), condition=%wide.region_21.22_spmd.clone.clone, body=%wide.region_11.21_spmd.clone.clone.sunk | while | flops 2628807680 | bytes 29113356 | solution.py:79
  708.5 9.3 fusion.282
  750.1 5.3 fusion.281
  781.1 9.3 fusion.282
  822.7 5.3 fusion.281
  853.7 9.3 fusion.282
  926.3 9.4 fusion.282
  980.1 9.4 fusion.176
  992.9 24.3 %all_to_all.69 = bf16[4,256,768]{1,2,0:T(8,128)(2,1)S(1)} all-to-all(bf16[4,256,768]{1,2,0:T(8,128)(2,1)S(1)} %fusion.161), channel_id=1, replica_groups=mesh['seq'=4,'grp'=2,'wsh'=4] {'seq'}, dimensions={0} | all-to-all | bytes 3145728 | tf_op jit(solution)/shard_map/all_to_all | solution.py:198
  1019.2 12.2 multiply_reduce_fusion.3
  1044.5 9.7 all_to_all.70
  1060.5 19.0 fusion.173
  1081.5 252.9 %reduce-scatter.11.cloned.1.call-done = f32[768,1536]{1,0:T(8,128)} async-done(((f32[3072,1536]{1,0:T(8,128)}), f32[768,1536]{1,0:T(8,128)}) %reduce-scatter.11.cloned.1.call-update) | async-done | bytes 4718608 | tf_op jit(solution)/shard_map/reduce_scatter | solution.py:96
  1334.4 651.6 %reduce-scatter.9.cloned.1.call-done = f32[384,6448]{0,1:T(8,128)} async-done(((f32[1536,6448]{0,1:T(8,128)}), f32[384,6448]{0,1:T(8,128)}) %reduce-scatter.9.cloned.1.call-update) | async-done | bytes 9904144 | tf_op jit(solution)/shard_map/reduce_scatter | solution.py:89
  1988.7 7.5 fusion.164
  1999.9 14.0 fusion.168
  2013.9 21.4 all-reduce.24
  2039.8 24.8 %all-reduce.22 = (f32[384]{0:T(512)}, f32[832,4]{0,1:T(4,128)}, f32[832]{0:T(1024)}, f32[12]{0:T(128)}, f32[12]{0:T(128)}, /*index=5*/f32[12]{0:T(128)}, f32[768]{0:T(1024)}) all-reduce(f32[384]{0:T(512)S(1)} %dynamic-slice.5, f32[832,4]{0,1:T(4,128)S(1)} %copy.193, ...), channel_id=1, replica_groups=mesh['seq'=4,'grp'=2,'wsh'=4] {'seq','grp'}, use_global_device_ids=true, to_apply=%region_26.27 | all-reduce | flops 5348 | bytes 42784 | tf_op jit(solution)/shard_map/psum | solution.py:98
  2064.6 163.0 %all-reduce.28.cloned.1.call-done = (f32[384,6448]{0,1:T(8,128)}, f32[768,1536]{1,0:T(8,128)}) async-done(((f32[384,6448]{0,1:T(8,128)}, f32[768,1536]{1,0:T(8,128)}), (f32[384,6448]{0,1:T(8,128)}, f32[768,1536]{1,0:T(8,128)})) %all-reduce.28.cloned.1.call-update) | async-done | bytes 14622736 | tf_op jit(solution)/shard_map/psum | solution.py:98
  2227.6 8.5 copy.389
  (612 shorter events, 531.8 us)
Async XLA Ops:
  7.2 15.5 copy-start.41
  7.2 343.1 %all-gather.6.cloned.1.call-start = ((), (), s32[]{:S(2)}) async-start(), calls=%async_computation.10 | async-start | bytes 24760320 | tf_op jit(solution)/shard_map/all_gather | solution.py:129
  7.9 513.5 %all-gather.8.cloned.1.call-start = ((), (), s32[]{:S(2)}) async-start(), calls=%async_computation.11 | async-start | bytes 11796480 | tf_op jit(solution)/shard_map/all_gather | solution.py:172
  8.9 13.7 copy-start.35
  9.0 351.7 %copy-start.37 = (f32[256]{0:T(256)}, f32[256]{0:T(256)S(1)}, u32[]{:S(2)}) copy-start(f32[256]{0:T(256)S(1)} %fusion.187) | copy-start | bytes 3076
  22.7 338.0 %copy-start.29 = (f32[1536]{0:T(1024)}, f32[1536]{0:T(1024)S(1)}, u32[]{:S(2)}) copy-start(f32[1536]{0:T(1024)S(1)} %reshape.483) | copy-start | bytes 18436
  37.5 329.9 %copy-start.46 = (u32[32]{0:T(128)S(1)}, u32[32]{0:T(128)}, u32[]{:S(2)}) copy-start(u32[32]{0:T(128)} %constant.226) | copy-start | bytes 388
  37.5 331.8 %copy-start.52 = (bf16[12]{0:T(256)(128)(2,1)S(1)}, bf16[12]{0:T(256)(128)(2,1)}, u32[]{:S(2)}) copy-start(bf16[12]{0:T(256)(128)(2,1)} %param.22) | copy-start | bytes 76
  37.5 332.0 %copy-start.53 = (bf16[12]{0:T(256)(128)(2,1)S(1)}, bf16[12]{0:T(256)(128)(2,1)}, u32[]{:S(2)}) copy-start(bf16[12]{0:T(256)(128)(2,1)} %param.23) | copy-start | bytes 76
  37.5 332.3 %copy-start.54 = (bf16[12]{0:T(256)(128)(2,1)S(1)}, bf16[12]{0:T(256)(128)(2,1)}, u32[]{:S(2)}) copy-start(bf16[12]{0:T(256)(128)(2,1)} %param.24) | copy-start | bytes 76
  37.5 332.5 %copy-start.47 = (bf16[832]{0:T(1024)(128)(2,1)S(1)}, bf16[832]{0:T(1024)(128)(2,1)}, u32[]{:S(2)}) copy-start(bf16[832]{0:T(1024)(128)(2,1)} %param.21) | copy-start | bytes 4996
  360.7 22.3 copy-start.6
  363.9 22.6 %collective-permute-start = (bf16[3,3328]{1,0:T(4,128)(2,1)S(1)}, bf16[3,3328]{1,0:T(4,128)(2,1)S(1)}, u32[]{:S(2)}, u32[]{:S(2)}) collective-permute-start(bf16[3,3328]{1,0:T(4,128)(2,1)S(1)} %copy.162), channel_id=1, source_target_pairs={{0,8},{8,16},{16,24},{1,9},{9,17},{17,25},{2,10},{10,18},{18,26},{... | collective-permute-start | bytes 59912 | tf_op jit(solution)/shard_map/ppermute | solution.py:17
  367.3 22.2 copy-start.21
  367.3 22.2 copy-start.23
  367.3 22.2 copy-start.25
  367.3 22.2 copy-start.27
  382.9 14.8 all-to-all-start
  397.8 35.0 %all-to-all-start.1 = ((bf16[256,4,768]{0,2,1:T(8,128)(2,1)}), bf16[256,4,768]{0,2,1:T(8,128)(2,1)}, u32[]{:S(2)}, u32[]{:S(2)}) async-start(bf16[256,4,768]{0,2,1:T(8,128)(2,1)} %bitcast.6), calls=%async_computation.1 | async-start | bytes 3145728 | tf_op jit(solution)/shard_map/all_to_all | solution.py:154
  492.7 23.6 %all-to-all-start.2 = ((bf16[4,256,768]{1,2,0:T(8,128)(2,1)}), bf16[4,256,768]{1,2,0:T(8,128)(2,1)}, u32[]{:S(2)}, u32[]{:S(2)}) async-start(bf16[4,256,768]{1,2,0:T(8,128)(2,1)} %fusion.162), calls=%async_computation.2 | async-start | bytes 3145728 | tf_op jit(solution)/shard_map/all_to_all | solution.py:169
  516.3 14.0 copy-start.15
  535.4 138.9 %all-to-all-start.3 = ((bf16[256,4,768]{0,2,1:T(8,128)(2,1)}), bf16[256,4,768]{0,2,1:T(8,128)(2,1)}, u32[]{:S(2)}, u32[]{:S(2)}) async-start(bf16[256,4,768]{0,2,1:T(8,128)(2,1)} %bitcast.595), calls=%async_computation.3 | async-start | bytes 3145728 | tf_op jit(solution)/shard_map/all_to_all | solution.py:189
  539.7 479.4 %reduce-scatter.7.cloned.1.call-start = ((), (), s32[]{:S(2)}) async-start(), calls=%async_computation.12 | async-start | bytes 1310720 | tf_op jit(solution)/shard_map/reduce_scatter | solution.py:196
  980.0 354.4 %reduce-scatter.11.cloned.1.call-start = ((), (), s32[]{:S(2)}) async-start(), calls=%async_computation.14 | async-start | bytes 23592960 | tf_op jit(solution)/shard_map/reduce_scatter | solution.py:96
  989.5 996.6 %reduce-scatter.9.cloned.1.call-start = ((), (), s32[]{:S(2)}) async-start(), calls=%async_computation.13 | async-start | bytes 49520640 | tf_op jit(solution)/shard_map/reduce_scatter | solution.py:89
  1019.2 12.3 copy-start.28
  1042.9 11.4 collective-permute-start.1
  1079.5 959.1 %reduce-scatter.13.cloned.1.call-start = ((), (), s32[]{:S(2)}) async-start(), calls=%async_computation.15 | async-start | bytes 2129920
  1081.4 1146.1 %all-reduce.28.cloned.1.call-start = ((), (), s32[]{:S(2)}) async-start(), calls=%async_computation.16 | async-start | bytes 29245440 | tf_op jit(solution)/shard_map/psum | solution.py:98
  1999.9 14.0 copy-start.34
  1999.9 35.8 %copy-start.36 = (f32[256]{0:T(256)S(1)}, f32[256]{0:T(256)}, u32[]{:S(2)}) copy-start(f32[256]{0:T(256)} %copy-done.35) | copy-start | bytes 3076
  1999.9 35.8 %copy-start.13 = (bf16[1,256,1536]{2,1,0:T(8,128)(2,1)S(1)}, bf16[1,256,1536]{2,1,0:T(8,128)(2,1)}, u32[]{:S(2)}) copy-start(bf16[1,256,1536]{2,1,0:T(8,128)(2,1)} %param.27) | copy-start | bytes 2359300
  (45 other events, 258.8 us)
Sparse Core Ops, SparseCore 0:
  9.6 340.6 all-gather.5
  351.9 166.4 all-gather.7
  980.1 36.9 reduce-scatter.6
  1019.4 315.0 reduce-scatter.10
  1336.6 649.3 reduce-scatter.8
  1988.8 40.4 reduce-scatter.12
  2033.1 194.4 all-reduce.27
where the time goes:
time: 2260 us; the launch traced here: 2250 us
  waiting for transfers between devices  1380 us (61%)
  matrix products  257 us (11%)
  local copies, waits for them, and re-layouts  225 us (10%)
  other arithmetic  176 us (8%)
  blocking collectives  163 us (7%)
    reduce_scatter x1, waiting for transfers between devices, reduce_grads(): lax.psum_scatter(grads[1], 'wsh', scatter_dimension=0, tiled=True)  652 us
    all_gather x1, waiting for transfers between devices, body(): lax.all_gather(in_weight, 'wsh', axis=0, tiled=True)  313 us
    reduce_scatter x1, waiting for transfers between devices, reduce_grads(): lax.psum_scatter(grads[8], 'wsh', scatter_dimension=0, tiled=True)  253 us
    psum x1, waiting for transfers between devices, reduce_grads(): lax.psum((shares[0], shares[1], shares[2], shares[3], shares[4], shares[5...  163 us
    dot_general x12, matrix products, advance(): result = jnp.einsum('hts,shp->thp', mixing, x_block, precision=highest)  77.1 us
    another operation x42, other arithmetic  46.3 us
  transfers between devices with their start and end apart: 13, of which 4 were waited for; matrix products, arithmetic and copies ran while one was open for 14% of the time, Pallas kernels for 0%

commit v1 on v0

--- a/solution.py
+++ b/solution.py
@@ -96,18 +96,21 @@
         lax.psum_scatter(grads[8], "wsh", scatter_dimension=0, tiled=True),
     )
     return lax.psum(
-        (
-            shares[0],
-            shares[1],
-            shares[2],
-            shares[3],
-            shares[4],
-            shares[5],
-            shares[6],
-            shares[7],
-            shares[8],
+        lax.psum(
+            (
+                shares[0],
+                shares[1],
+                shares[2],
+                shares[3],
+                shares[4],
+                shares[5],
+                shares[6],
+                shares[7],
+                shares[8],
+            ),
+            "grp",
         ),
-        ("seq", "grp"),
+        "seq",
     )
 
 

time: 2260 us -> 2420 us (1.071)
  waiting for transfers between devices: 1380 us -> 1530 us
    psum x0 -> x1, waiting for transfers between devices: none -> 245 us  [reduce_grads(): lax.psum(lax.psum((shares[0], shares[1], shares[2], shares[3], shares[4],...]
    psum x1, waiting for transfers between devices: 163 us -> 56.5 us  [reduce_grads(): lax.psum((shares[0], shares[1], shares[2], shares[3], shares[4], shares[5...]
  transfers between devices with their start and end apart: 13 -> 14, of which waited for: 4 -> 6; matrix products, arithmetic and copies ran while one was open for 14% -> 14% of each run, Pallas kernels for 0% -> 0%
where the time goes in v1:
time: 2420 us; the launch traced here: 2410 us
  waiting for transfers between devices  1530 us (63%)
  matrix products  253 us (10%)
  local copies, waits for them, and re-layouts  239 us (10%)
  other arithmetic  180 us (7%)
  blocking collectives  155 us (6%)
    reduce_scatter x1, waiting for transfers between devices, reduce_grads(): lax.psum_scatter(grads[1], 'wsh', scatter_dimension=0, tiled=True)  652 us
    all_gather x1, waiting for transfers between devices, body(): lax.all_gather(in_weight, 'wsh', axis=0, tiled=True)  314 us
    reduce_scatter x1, waiting for transfers between devices, reduce_grads(): lax.psum_scatter(grads[8], 'wsh', scatter_dimension=0, tiled=True)  255 us
    psum x1, waiting for transfers between devices, reduce_grads(): lax.psum(lax.psum((shares[0], shares[1], shares[2], shares[3], shares[4],...  245 us
    dot_general x12, matrix products, advance(): result = jnp.einsum('hts,shp->thp', mixing, x_block, precision=highest)  77 us
    another operation x73, local copies, waits for them, and re-layouts  59.2 us
    psum x1, waiting for transfers between devices, reduce_grads(): lax.psum((shares[0], shares[1], shares[2], shares[3], shares[4], shares[5...  56.5 us
    another operation x42, other arithmetic  52.6 us
  transfers between devices with their start and end apart: 14, of which 6 were waited for; matrix products, arithmetic and copies ran while one was open for 14% of the time, Pallas kernels for 0%

profile of v1, /device:TPU:0, one launch (start us, length us, event | category | flops | bytes accessed | tf_op | source)
XLA Modules:
  0.0 2405.4 jit_solution(1155109353591857116)
XLA Ops:
  9.0 13.6 all-gather
  22.7 13.5 all-gather.1
  36.7 313.6 %all-gather.6.cloned.1.call-done = bf16[1536,6448]{0,1:T(8,128)(2,1)} async-done(((bf16[384,6448]{0,1:T(8,128)(2,1)}), bf16[1536,6448]{0,1:T(8,128)(2,1)}) %all-gather.6.cloned.1.call-update) | async-done | bytes 19808272 | tf_op jit(solution)/shard_map/all_gather | solution.py:132
  350.3 11.5 convolution_convert_fusion
  370.8 10.2 all-reduce.27
  386.8 7.0 multiply_convert_fusion
  401.2 26.7 %all_gather.36 = bf16[1024,256]{0,1:T(8,128)(2,1)S(1)} all-gather(bf16[256,256]{0,1:T(8,128)(2,1)S(1)} %slice.146), channel_id=1, replica_groups=mesh['seq'=4,'grp'=2,'wsh'=4] {'seq'}, dimensions={0}, use_global_device_ids=true | all-gather | bytes 655360 | tf_op jit(solution)/shard_map/all_gather | solution.py:160
  433.8 71.6 %while.86 = (s32[]{:T(128)}, f32[12,128,64]{1,2,0:T(8,128)S(1)}, f32[4,256,12,64]{1,3,2,0:T(8,128)}, f32[4,256,12]{1,2,0:T(8,128)}, f32[4,256,12]{1,2,0:T(8,128)...) while((s32[]{:T(128)}, f32[12,128,64]{1,2,0:T(8,128)S(1)}, ...), condition=%wide.region_4.5_spmd.clone.clone, body=%wide.region_1.4_spmd.clone.clone.sunk | while | flops 1313970176 | bytes 7889523 | solution.py:79
  514.0 13.8 all-gather.2
  537.0 8.6 multiply_reduce_fusion.4
  561.1 128.2 %while.87 = (s32[]{:T(128)}, f32[12,128,64]{1,2,0:T(8,128)}, f32[4,128,256]{1,2,0:T(8,128)}, f32[4,12,256,256]{3,2,1,0:T(8,128)}, f32[4,1,256,256]{3,2,1,0:T(8,1...) while((s32[]{:T(128)}, f32[12,128,64]{1,2,0:T(8,128)}, ...), condition=%wide.region_10.11_spmd.clone.clone, body=%wide.region_7.10_spmd.clone.clone.sunk | while | flops 709793792 | bytes 22214624 | solution.py:79
  697.5 300.1 %while.88 = (s32[]{:T(128)}, f32[12,128,64]{1,2,0:T(8,128)S(1)}, f32[4,256,12,64]{1,3,2,0:T(8,128)}, f32[4,256,12]{1,2,0:T(8,128)}, f32[4,256,12]{1,2,0:T(8,128)...) while((s32[]{:T(128)}, f32[12,128,64]{1,2,0:T(8,128)S(1)}, ...), condition=%wide.region_21.22_spmd.clone.clone, body=%wide.region_11.21_spmd.clone.clone.sunk | while | flops 2628807680 | bytes 29113356 | solution.py:79
  732.8 9.3 fusion.282
  805.3 9.3 fusion.282
  847.0 5.3 fusion.281
  877.9 9.3 fusion.282
  950.5 9.3 fusion.282
  992.1 5.3 fusion.281
  1004.2 9.5 fusion.176
  1017.3 25.5 %all_to_all.69 = bf16[4,256,768]{1,2,0:T(8,128)(2,1)S(1)} all-to-all(bf16[4,256,768]{1,2,0:T(8,128)(2,1)S(1)} %fusion.161), channel_id=1, replica_groups=mesh['seq'=4,'grp'=2,'wsh'=4] {'seq'}, dimensions={0} | all-to-all | bytes 3145728 | tf_op jit(solution)/shard_map/all_to_all | solution.py:201
  1044.8 12.5 multiply_reduce_fusion.3
  1070.5 9.2 all_to_all.70
  1085.9 17.2 fusion.173
  1103.1 255.0 %reduce-scatter.11.cloned.1.call-done = f32[768,1536]{1,0:T(8,128)} async-done(((f32[3072,1536]{1,0:T(8,128)}), f32[768,1536]{1,0:T(8,128)}) %reduce-scatter.11.cloned.1.call-update) | async-done | bytes 4718608 | tf_op jit(solution)/shard_map/reduce_scatter | solution.py:96
  1358.2 651.6 %reduce-scatter.9.cloned.1.call-done = f32[384,6448]{0,1:T(8,128)} async-done(((f32[1536,6448]{0,1:T(8,128)}), f32[384,6448]{0,1:T(8,128)}) %reduce-scatter.9.cloned.1.call-update) | async-done | bytes 9904144 | tf_op jit(solution)/shard_map/reduce_scatter | solution.py:89
  2011.8 56.5 %all-reduce.33.cloned.1.call-done = (f32[384,6448]{0,1:T(8,128)}, f32[768,1536]{1,0:T(8,128)}) async-done(((f32[384,6448]{0,1:T(8,128)}, f32[768,1536]{1,0:T(8,128)}), (f32[384,6448]{0,1:T(8,128)}, f32[768,1536]{1,0:T(8,128)})) %all-reduce.33.cloned.1.call-update) | async-done | bytes 14622736 | tf_op jit(solution)/shard_map/psum | solution.py:99
  2070.9 7.4 fusion.164
  2081.8 13.9 fusion.168
  2095.7 21.0 all-reduce.22
  2124.8 18.2 all-reduce.23
  2142.9 244.7 %all-reduce.31.cloned.1.call-done = (f32[384,6448]{0,1:T(8,128)}, f32[768,1536]{1,0:T(8,128)}) async-done(((f32[384,6448]{0,1:T(8,128)}, f32[768,1536]{1,0:T(8,128)}), (f32[384,6448]{0,1:T(8,128)}, f32[768,1536]{1,0:T(8,128)})) %all-reduce.31.cloned.1.call-update) | async-done | bytes 14622736 | tf_op jit(solution)/shard_map/psum | solution.py:98
  2387.6 8.5 copy.391
  (610 shorter events, 558.7 us)
Async XLA Ops:
  7.2 343.1 %all-gather.6.cloned.1.call-start = ((), (), s32[]{:S(2)}) async-start(), calls=%async_computation.10 | async-start | bytes 24760320 | tf_op jit(solution)/shard_map/all_gather | solution.py:132
  7.9 529.0 %all-gather.8.cloned.1.call-start = ((), (), s32[]{:S(2)}) async-start(), calls=%async_computation.11 | async-start | bytes 11796480 | tf_op jit(solution)/shard_map/all_gather | solution.py:175
  9.0 352.8 %copy-start.36 = (f32[256]{0:T(256)}, f32[256]{0:T(256)S(1)}, u32[]{:S(2)}) copy-start(f32[256]{0:T(256)S(1)} %fusion.187) | copy-start | bytes 3076
  22.7 339.2 %copy-start.28 = (f32[1536]{0:T(1024)}, f32[1536]{0:T(1024)S(1)}, u32[]{:S(2)}) copy-start(f32[1536]{0:T(1024)S(1)} %reshape.483) | copy-start | bytes 18436
  36.6 325.2 %copy-start.11 = (bf16[256,1536]{1,0:T(8,128)(2,1)}, bf16[256,1536]{1,0:T(8,128)(2,1)S(1)}, u32[]{:S(2)}) copy-start(bf16[256,1536]{1,0:T(8,128)(2,1)S(1)} %fusion.167) | copy-start | bytes 2359300
  36.6 331.3 %copy-start.45 = (u32[32]{0:T(128)S(1)}, u32[32]{0:T(128)}, u32[]{:S(2)}) copy-start(u32[32]{0:T(128)} %constant.226) | copy-start | bytes 388
  36.6 333.2 %copy-start.51 = (bf16[12]{0:T(256)(128)(2,1)S(1)}, bf16[12]{0:T(256)(128)(2,1)}, u32[]{:S(2)}) copy-start(bf16[12]{0:T(256)(128)(2,1)} %param.22) | copy-start | bytes 76
  36.6 333.4 %copy-start.52 = (bf16[12]{0:T(256)(128)(2,1)S(1)}, bf16[12]{0:T(256)(128)(2,1)}, u32[]{:S(2)}) copy-start(bf16[12]{0:T(256)(128)(2,1)} %param.23) | copy-start | bytes 76
  36.6 333.6 %copy-start.53 = (bf16[12]{0:T(256)(128)(2,1)S(1)}, bf16[12]{0:T(256)(128)(2,1)}, u32[]{:S(2)}) copy-start(bf16[12]{0:T(256)(128)(2,1)} %param.24) | copy-start | bytes 76
  36.7 333.9 %copy-start.46 = (bf16[832]{0:T(1024)(128)(2,1)S(1)}, bf16[832]{0:T(1024)(128)(2,1)}, u32[]{:S(2)}) copy-start(bf16[832]{0:T(1024)(128)(2,1)} %param.21) | copy-start | bytes 4996
  363.8 21.9 slice-start.1
  364.2 21.0 collective-permute-start
  367.8 19.0 copy-start.20
  367.8 19.0 copy-start.22
  367.8 19.0 copy-start.24
  367.8 19.0 copy-start.26
  381.6 13.4 all-to-all-start
  395.1 33.0 %copy-start.16 = (bf16[256,4,12]{0,2,1:T(8,128)(2,1)}, bf16[256,4,12]{0,2,1:T(8,128)(2,1)S(1)}, u32[]{:S(2)}) copy-start(bf16[256,4,12]{0,2,1:T(8,128)(2,1)S(1)} %all-to-all-done) | copy-start | bytes 73732
  395.1 35.0 %all-to-all-start.1 = ((bf16[256,4,768]{0,2,1:T(8,128)(2,1)}), bf16[256,4,768]{0,2,1:T(8,128)(2,1)}, u32[]{:S(2)}, u32[]{:S(2)}) async-start(bf16[256,4,768]{0,2,1:T(8,128)(2,1)} %bitcast.595), calls=%async_computation.1 | async-start | bytes 3145728 | tf_op jit(solution)/shard_map/all_to_all | solution.py:157
  399.4 30.6 %copy-start.49 = (f32[48]{0:T(128)}, f32[48]{0:T(128)S(1)}, u32[]{:S(2)}) copy-start(f32[48]{0:T(128)S(1)} %convert_element_type.162) | copy-start | bytes 580
  399.5 30.6 %copy-start.41 = (f32[12]{0:T(128)}, f32[12]{0:T(128)S(1)}, u32[]{:S(2)}) copy-start(f32[12]{0:T(128)S(1)} %dynamic_slice.266) | copy-start | bytes 148
  400.4 29.7 %copy-start.43 = (f32[12]{0:T(128)}, f32[12]{0:T(128)S(1)}, u32[]{:S(2)}) copy-start(f32[12]{0:T(128)S(1)} %fusion.189) | copy-start | bytes 148
  509.3 22.5 all-to-all-start.2
  550.6 138.7 %all-to-all-start.3 = ((bf16[256,4,768]{0,2,1:T(8,128)(2,1)}), bf16[256,4,768]{0,2,1:T(8,128)(2,1)}, u32[]{:S(2)}, u32[]{:S(2)}) async-start(bf16[256,4,768]{0,2,1:T(8,128)(2,1)} %bitcast.596), calls=%async_computation.3 | async-start | bytes 3145728 | tf_op jit(solution)/shard_map/all_to_all | solution.py:192
  554.9 489.9 %reduce-scatter.7.cloned.1.call-start = ((), (), s32[]{:S(2)}) async-start(), calls=%async_computation.12 | async-start | bytes 1310720 | tf_op jit(solution)/shard_map/reduce_scatter | solution.py:199
  1004.2 354.0 %reduce-scatter.11.cloned.1.call-start = ((), (), s32[]{:S(2)}) async-start(), calls=%async_computation.14 | async-start | bytes 23592960 | tf_op jit(solution)/shard_map/reduce_scatter | solution.py:96
  1013.7 996.1 %reduce-scatter.9.cloned.1.call-start = ((), (), s32[]{:S(2)}) async-start(), calls=%async_computation.13 | async-start | bytes 49520640 | tf_op jit(solution)/shard_map/reduce_scatter | solution.py:89
  1068.9 10.8 collective-permute-start.1
  1103.1 965.2 %all-reduce.33.cloned.1.call-start = ((), (), s32[]{:S(2)}) async-start(), calls=%async_computation.17 | async-start | bytes 29245440 | tf_op jit(solution)/shard_map/psum | solution.py:99
  2009.8 110.3 %reduce-scatter.13.cloned.1.call-start = ((), (), s32[]{:S(2)}) async-start(), calls=%async_computation.15 | async-start | bytes 2129920
  2011.8 375.9 %all-reduce.31.cloned.1.call-start = ((), (), s32[]{:S(2)}) async-start(), calls=%async_computation.16 | async-start | bytes 29245440 | tf_op jit(solution)/shard_map/psum | solution.py:98
  2081.7 35.4 %copy-start.35 = (f32[256]{0:T(256)S(1)}, f32[256]{0:T(256)}, u32[]{:S(2)}) copy-start(f32[256]{0:T(256)} %copy-done.34) | copy-start | bytes 3076
  (44 other events, 337.6 us)
Sparse Core Ops, SparseCore 0:
  9.6 340.6 all-gather.5
  351.9 166.2 all-gather.7
  1004.3 38.3 reduce-scatter.6
  1044.8 313.2 reduce-scatter.10
  1360.4 649.3 reduce-scatter.8
  2012.2 56.0 all-reduce.32
  2071.2 39.5 reduce-scatter.12
  2114.5 273.0 all-reduce.30
